TPU v7x, 32 devices: a whole 2x2x4 slice. The times are simulated.
32 devices in a mesh: grp: 2 (over x), seq: 16 (over z, y, core).
Axes of the slice: x: 2, y: 2, z: 4, core: 2. Of those that a mesh axis runs over, the one named last changes fastest.
Arguments:
- alignment: bfloat16 [64, 128, 768], P(('grp', 'seq')), parts along dimension 0, may hold values from -20 to 20
- protein_id: int32 [256], P('grp'), parts along dimension 0, may hold values from 0 to 3, never falling along the last dimension, each value on 1 to 64 neighbouring positions
- row_depth: int32 [8], P('grp'), parts along dimension 0, may hold values from 8 to 32, as said below
- row_gain: float32 [768], replicated, may hold values from 0.1 to 1.9
- row_query: bfloat16 [768, 768], replicated, may hold values from -40 to 40
- row_key: bfloat16 [768, 768], replicated, may hold values from -0.21875 to 0.21875
- row_value: bfloat16 [768, 768], replicated, may hold values from -0.21875 to 0.21875
- row_output: bfloat16 [768, 768], replicated, may hold values from -0.21875 to 0.21875
- column_gain: float32 [768], replicated, may hold values from 0.1 to 1.9
- column_query: bfloat16 [768, 768], replicated, may hold values from -40 to 40
- column_key: bfloat16 [768, 768], replicated, may hold values from -0.21875 to 0.21875
- column_value: bfloat16 [768, 768], replicated, may hold values from -0.21875 to 0.21875
- column_output: bfloat16 [768, 768], replicated, may hold values from -0.21875 to 0.21875
Outputs:
- layer_out: bfloat16 [64, 128, 768], P(('grp', 'seq')), parts along dimension 0
There are 2 independent parts, one for each index of `grp`. A program takes and returns all parts, laid end to end along the dimension named above; an argument that names none is the same for every part. Nothing has to cross between parts.
Inputs may be any that keep to these rules, and one draw needn't show every extreme that they name: `row_depth`: row 0 is real for every protein; one protein of each pack has all 32 rows real. `protein_id`: proteins occupy contiguous column ranges in order, each 1 to 64 columns.
All inputs are finite; a program needn't handle non-finite values.
Results may differ from a plain program's by a relative error of at most 0.011.
Values may be sent and summed in bfloat16 or wider, within the bound.
No kernel may reach another device: no remote copies, remote signals or barrier semaphores. Data moves between devices by JAX's collectives and lax.ppermute only.
A program may use at most 64 MiB of HBM per device.

v0:
```python
import math
import jax
import jax.numpy as jnp
from jax import lax
from jax.sharding import PartitionSpec as P

H = 12


def layer_norm(values, gain):
    full = values.astype(jnp.float32)
    middle = jnp.mean(full, axis=-1, keepdims=True)
    spread = jnp.mean((full - middle) ** 2, axis=-1, keepdims=True)
    return ((full - middle) * lax.rsqrt(spread + 1e-05) * gain).astype(jnp.bfloat16)


def project(normed, weight):
    shape = normed.shape
    flattened = normed.reshape(-1, shape[-1])
    return (
        jnp.dot(flattened, weight, preferred_element_type=jnp.float32)
        .astype(jnp.bfloat16)
        .reshape(shape[:-1] + (weight.shape[1],))
    )


def column_depth(protein_id, row_depth):
    onehot = protein_id[:, None] == jnp.arange(row_depth.shape[0], dtype=jnp.int32)[None, :]
    return jnp.sum(jnp.where(onehot, row_depth[None, :], 0), axis=1)


def per_device(
    alignment,
    protein_id,
    row_depth,
    row_gain,
    row_query,
    row_key,
    row_value,
    row_output,
    column_gain,
    column_query,
    column_key,
    column_value,
    column_output,
):
    rows_dev, columns, width = alignment.shape
    devices = lax.axis_size("seq")
    position = lax.axis_index("seq")
    total_rows = rows_dev * devices
    head_count = H
    head_size = width // head_count
    tile_cols = columns // devices
    depth_col = column_depth(protein_id, row_depth)
    row_ids = position * rows_dev + jnp.arange(rows_dev, dtype=jnp.int32)
    valid = row_ids[:, None] < depth_col[None, :]
    mask_bf = valid.astype(jnp.bfloat16)[:, :, None]
    normed_row = layer_norm(alignment, row_gain)
    query_a = (project(normed_row, row_query) * mask_bf).reshape(
        rows_dev, columns, head_count, head_size
    )
    key_a = (project(normed_row, row_key) * mask_bf).reshape(
        rows_dev, columns, head_count, head_size
    )
    value_a = project(normed_row, row_value).reshape(rows_dev, columns, head_count, head_size)
    scale = 1.0 / (math.sqrt(head_size) * math.sqrt(total_rows))
    tied = (
        lax.psum_scatter(
            jnp.einsum("rihe,rjhe->ihj", query_a, key_a, preferred_element_type=jnp.float32),
            "seq",
            scatter_dimension=0,
            tiled=True,
        )
        * scale
    )
    prot_query = lax.dynamic_slice_in_dim(protein_id, position * tile_cols, tile_cols, 0)
    same_prot = prot_query[:, None, None] == protein_id[None, None, :]
    tied = jnp.where(same_prot, tied, -1000000000.0)
    row_weights = jax.nn.softmax(tied, axis=-1).astype(jnp.bfloat16)
    row_mixed = (
        jnp.einsum(
            "ihj,rjhe->rihe",
            lax.all_gather(row_weights, "seq", axis=0, tiled=True),
            value_a,
            preferred_element_type=jnp.float32,
        )
        .astype(jnp.bfloat16)
        .reshape(rows_dev, columns, width)
    )
    after_row = (
        alignment.astype(jnp.float32)
        + jnp.dot(
            row_mixed.reshape(-1, width), row_output, preferred_element_type=jnp.float32
        ).reshape(rows_dev, columns, width)
    ).astype(jnp.bfloat16)
    normed_col = layer_norm(after_row, column_gain)
    moved = lax.all_to_all(normed_col, "seq", split_axis=1, concat_axis=0, tiled=True)
    query_b = project(moved, column_query)
    key_b = project(moved, column_key)
    value_b = project(moved, column_value)
    query_b = query_b.reshape(total_rows, tile_cols, head_count, head_size)
    key_b = key_b.reshape(total_rows, tile_cols, head_count, head_size)
    value_b = value_b.reshape(total_rows, tile_cols, head_count, head_size)
    depth_tile = lax.dynamic_slice_in_dim(depth_col, position * tile_cols, tile_cols, 0)
    key_valid = jnp.arange(total_rows, dtype=jnp.int32)[None, :] < depth_tile[:, None]
    col_scores = jnp.einsum(
        "rche,sche->chrs", query_b, key_b, preferred_element_type=jnp.float32
    ) / math.sqrt(head_size)
    col_scores = jnp.where(key_valid[:, None, None, :], col_scores, -1000000000.0)
    col_weights = jax.nn.softmax(col_scores, axis=-1).astype(jnp.bfloat16)
    col_mixed = jnp.einsum(
        "chrs,sche->rche", col_weights, value_b, preferred_element_type=jnp.float32
    ).astype(jnp.bfloat16)
    col_mixed = col_mixed.reshape(total_rows, tile_cols, width)
    returned = lax.all_to_all(col_mixed, "seq", split_axis=0, concat_axis=1, tiled=True)
    layer_out = after_row.astype(jnp.float32) + jnp.dot(
        returned.reshape(-1, width), column_output, preferred_element_type=jnp.float32
    ).reshape(rows_dev, columns, width)
    return layer_out.astype(jnp.bfloat16)


def solution(mesh):
    return jax.shard_map(
        per_device,
        mesh=mesh,
        in_specs=(
            P(("grp", "seq"), None, None),
            P("grp"),
            P("grp"),
            P(),
            P(),
            P(),
            P(),
            P(),
            P(),
            P(),
            P(),
            P(),
            P(),
        ),
        out_specs=P(("grp", "seq"), None, None),
        check_vma=False,
    )
```

profile of v0, /device:TPU:0, one launch (start us, length us, event | category | flops | bytes accessed | tf_op | source)
XLA Modules:
  0.0 158.1 jit_solution(10954076205752719301)
XLA Ops:
  6.5 1.3 convert_reduce_fusion
  7.8 1.2 fusion.15
  9.1 1.2 fusion.17
  11.1 1.7 %convolution_convert_fusion.4 = bf16[256,768]{1,0:T(8,128)(2,1)S(1)} fusion(bf16[256,768]{1,0:T(8,128)(2,1)S(1)} %bitcast.61, bf16[768,768]{1,0:T(8,128)(2,1)} %param.17), kind=kOutput, calls=%fused_computation.17 | convolution fusion | flops 302186496 | bytes 1966080 | tf_op jit(solution)/shard_map/dot_general | solution.py:21
  14.1 1.4 copy.79
  15.6 0.5 convolution_convert_fusion.6
  16.4 59.4 %reduce-scatter.2.cloned.1.call-done = f32[8,12,128]{2,1,0:T(8,128)} async-done(((f32[128,12,128]{2,1,0:T(8,128)}), f32[8,12,128]{2,1,0:T(8,128)}) %reduce-scatter.2.cloned.1.call-update) | async-done | bytes 49168 | tf_op jit(solution)/shard_map/reduce_scatter | solution.py:68
  75.8 1.0 fusion.38
  76.9 20.5 %all_gather.3 = bf16[128,12,128]{2,0,1:T(8,128)(2,1)S(1)} all-gather(bf16[8,12,128]{2,0,1:T(8,128)(2,1)S(1)} %copy.80), channel_id=1, replica_groups=mesh['grp'=2,'seq'=16] {'seq'}, dimensions={0}, use_global_device_ids=true | all-gather | bytes 417792 | tf_op jit(solution)/shard_map/all_gather | solution.py:83
  97.9 0.6 fusion.39
  99.0 1.2 copy.84
  100.1 3.6 %all-to-all-start = ((bf16[2,128,768]{2,0,1:T(2,128)(2,1)}), bf16[2,128,768]{2,0,1:T(2,128)(2,1)S(1)}, u32[]{:S(2)}, u32[]{:S(2)}) async-start(bf16[2,128,768]{2,0,1:T(2,128)(2,1)} %copy.84), calls=%async_computation.1 | async-start | bytes 786432 | tf_op jit(solution)/shard_map/all_to_all | solution.py:97
  103.8 12.0 %all-to-all-done = bf16[2,128,768]{2,0,1:T(2,128)(2,1)S(1)} async-done(((bf16[2,128,768]{2,0,1:T(2,128)(2,1)}), bf16[2,128,768]{2,0,1:T(2,128)(2,1)S(1)}, u32[]{:S(2)}, u32[]{:S(2)}) %all-to-all-start) | async-done | bytes 393248 | tf_op jit(solution)/shard_map/all_to_all | solution.py:97
  115.9 1.7 %convolution_convert_fusion.2 = bf16[256,768]{1,0:T(8,128)(2,1)S(1)} fusion(bf16[256,768]{1,0:T(8,128)(2,1)S(1)} %bitcast.63, bf16[768,768]{1,0:T(8,128)(2,1)} %param.22), kind=kOutput, calls=%fused_computation.15 | convolution fusion | flops 302186496 | bytes 1966080 | tf_op jit(solution)/shard_map/dot_general | solution.py:21
  117.7 1.6 %reshape_reshape.15 = bf16[32,8,12,64]{3,2,1,0:T(8,128)(2,1)} reshape(bf16[256,768]{1,0:T(8,128)(2,1)S(1)} %convolution_convert_fusion.2) | data formatting | bytes 786432 | tf_op jit(solution)/shard_map/reshape;reshape | solution.py:101
  119.3 1.7 %convolution_convert_fusion.1 = bf16[256,768]{1,0:T(8,128)(2,1)S(1)} fusion(bf16[256,768]{1,0:T(8,128)(2,1)S(1)} %bitcast.64, bf16[768,768]{1,0:T(8,128)(2,1)} %param.23), kind=kOutput, calls=%fused_computation.14 | convolution fusion | flops 302186496 | bytes 1966080 | tf_op jit(solution)/shard_map/dot_general | solution.py:21
  121.0 1.6 reshape_reshape.16
  122.6 1.7 %convolution_convert_fusion.3 = bf16[256,768]{1,0:T(8,128)(2,1)S(1)} fusion(bf16[256,768]{1,0:T(8,128)(2,1)S(1)} %bitcast.65, bf16[768,768]{1,0:T(8,128)(2,1)} %param.24), kind=kOutput, calls=%fused_computation.16 | convolution fusion | flops 302186496 | bytes 1966080 | tf_op jit(solution)/shard_map/dot_general | solution.py:21
  124.3 1.6 reshape_reshape.14
  125.9 4.2 %fusion.40 = (f32[8,12,32]{2,1,0:T(8,128)S(1)}, f32[8,12,32,32]{2,3,1,0:T(8,128)}) fusion(bf16[32,8,12,64]{3,2,1,0:T(8,128)(2,1)} %reshape_reshape.16, bf16[32,8,12,64]{3,2,1,0:T(8,128)(2,1)} %reshape_reshape.15, pred[8,32]{1,0:T(8,128)(4,1)S(1)} %iota_compare_fusion), kind=kOutput, calls=%fused_computation.68 | convolution fusion | flops 12976159 | bytes 1192192 | tf_op jit(solution)/shard_map/sub | solution.py:110
  130.1 2.1 %fusion.4 = bf16[32,8,12,64]{3,0,2,1:T(8,128)(2,1)S(1)} fusion(f32[8,12,32,32]{2,3,1,0:T(8,128)} %get-tuple-element.12, bf16[32,8,12,64]{3,2,1,0:T(8,128)(2,1)S(1)} %copy-done.4, f32[8,12,32]{2,1,0:T(8,128)S(1)} %get-tuple-element.11), kind=kOutput, calls=%fused_computation.7 | convolution fusion | flops 12976128 | bytes 1191936 | tf_op jit(solution)/shard_map/chrs,sche->rche/dot_general | solution.py:111
  132.6 0.6 reshape.144
  133.3 15.5 %all_to_all.30 = bf16[32,8,768]{2,1,0:T(8,128)(2,1)S(1)} all-to-all(bf16[32,8,768]{2,1,0:T(8,128)(2,1)S(1)} %reshape.144), channel_id=1, replica_groups=mesh['grp'=2,'seq'=16] {'seq'}, dimensions={0} | all-to-all | bytes 786432 | tf_op jit(solution)/shard_map/all_to_all | solution.py:115
  148.7 2.5 %fusion.7 = bf16[2,128,768]{2,1,0:T(8,128)(2,1)} fusion(f32[2,128,768]{2,1,0:T(8,128)S(1)} %get-tuple-element.10, bf16[768,768]{1,0:T(8,128)(2,1)} %param.25, bf16[2,16,8,768]{3,2,0,1:T(8,128)(2,1)S(1)} %bitcast.72), kind=kOutput, calls=%fused_computation.13 | convolution fusion | flops 302383104 | bytes 2752512 | tf_op jit(solution)/shard_map/dot_general | solution.py:116
  (48 shorter events, 3.9 us)
Async XLA Ops:
  6.5 91.4 %copy-start = (bf16[768,768]{1,0:T(8,128)(2,1)S(1)}, bf16[768,768]{1,0:T(8,128)(2,1)}, u32[]{:S(2)}) copy-start(bf16[768,768]{1,0:T(8,128)(2,1)} %param.20) | copy-start | bytes 3538948
  6.5 3.8 %copy-start.2 = (bf16[768,768]{1,0:T(8,128)(2,1)S(1)}, bf16[768,768]{1,0:T(8,128)(2,1)}, u32[]{:S(2)}) copy-start(bf16[768,768]{1,0:T(8,128)(2,1)} %param.18) | copy-start | bytes 3538948
  6.5 69.2 %reduce-scatter.2.cloned.1.call-start = ((), (), s32[]{:S(2)}) async-start(), calls=%async_computation.3 | async-start | bytes 1114112 | tf_op jit(solution)/shard_map/reduce_scatter | solution.py:68
  12.8 0.7 copy-start.6
  12.8 0.7 copy-start.7
  14.1 1.5 copy-start.3
  76.9 21.0 %copy-start.1 = (bf16[2,128,768]{2,1,0:T(8,128)(2,1)S(1)}, bf16[2,128,768]{2,1,0:T(8,128)(2,1)}, u32[]{:S(2)}) copy-start(bf16[2,128,768]{2,1,0:T(8,128)(2,1)} %param.13) | copy-start | bytes 1179652
  97.9 0.8 copy-start.5
  100.1 15.7 %all-to-all-start = ((bf16[2,128,768]{2,0,1:T(2,128)(2,1)}), bf16[2,128,768]{2,0,1:T(2,128)(2,1)S(1)}, u32[]{:S(2)}, u32[]{:S(2)}) async-start(bf16[2,128,768]{2,0,1:T(2,128)(2,1)} %copy.84), calls=%async_computation.1 | async-start | bytes 786432 | tf_op jit(solution)/shard_map/all_to_all | solution.py:97
  125.9 4.2 %copy-start.4 = (bf16[32,8,12,64]{3,2,1,0:T(8,128)(2,1)S(1)}, bf16[32,8,12,64]{3,2,1,0:T(8,128)(2,1)}, u32[]{:S(2)}) copy-start(bf16[32,8,12,64]{3,2,1,0:T(8,128)(2,1)} %reshape_reshape.14) | copy-start | bytes 1179652
Sparse Core Ops, SparseCore 0:
  15.6 60.1 reduce-scatter.1
where the time goes:
time: 159 us; the launch traced here: 158 us
  waiting for transfers between devices  71.4 us (45%)
  blocking collectives  36 us (23%)
  matrix products  18.1 us (11%)
  between operations  13.7 us (9%)
  local copies, waits for them, and re-layouts  9.7 us (6%)
  other arithmetic  5.64 us (4%)
  starting transfers between devices  3.56 us (2%)
    reduce_scatter x1, waiting for transfers between devices, per_device(): lax.psum_scatter(jnp.einsum('rihe,rjhe->ihj', query_a, key_a, preferred_e...  59.4 us
    all_gather x1, blocking collectives, per_device(): lax.all_gather(row_weights, 'seq', axis=0, tiled=True)  20.5 us
    all_to_all x1, blocking collectives, per_device(): lax.all_to_all(col_mixed, 'seq', split_axis=0, concat_axis=1, tiled=True)  15.5 us
    all_to_all x1, waiting for transfers between devices, per_device(): lax.all_to_all(normed_col, 'seq', split_axis=1, concat_axis=0, tiled=True)  12 us
    dot_general x6, matrix products, project(): jnp.dot(flattened, weight, preferred_element_type=jnp.float32)  7.94 us
    sub x1, matrix products, per_device(): col_weights = jax.nn.softmax(col_scores, axis=-1).astype(jnp.bfloat16)  4.24 us
    all_to_all x1, starting transfers between devices, per_device(): lax.all_to_all(normed_col, 'seq', split_axis=1, concat_axis=0, tiled=True)  3.55 us
  transfers between devices with their start and end apart: 2, of which 2 were waited for; matrix products, arithmetic and copies ran while one was open for 1% of the time, Pallas kernels for 0%

commit v1 on v0

--- a/solution.py
+++ b/solution.py
@@ -5,6 +5,28 @@
 from jax.sharding import PartitionSpec as P
 
 H = 12
+
+
+def joined_along(blocks, dim):
+    blocks = jnp.moveaxis(blocks, 0, dim)
+    dims = blocks.shape
+    return blocks.reshape(*dims[:dim], dims[dim] * dims[dim + 1], *dims[dim + 2 :])
+
+
+def collect(value, axis, dim):
+    length = lax.axis_size(axis)
+    pairs = [(i, (i + 1) % length) for i in range(length)]
+    back = [(b, a) for a, b in pairs]
+    lower, upper = ([], [])
+    for step in range(length - 1):
+        if step % 2 == 0:
+            lower.append(lax.ppermute(lower[-1] if lower else value, axis, pairs))
+        else:
+            upper.append(lax.ppermute(upper[-1] if upper else value, axis, back))
+    blocks = jnp.stack([*lower[::-1], value, *upper])
+    shift = lax.axis_index(axis) - len(lower)
+    blocks = blocks[(jnp.arange(length) - shift) % length]
+    return joined_along(blocks, dim)
 
 
 def layer_norm(values, gain):
@@ -80,7 +102,7 @@
     row_mixed = (
         jnp.einsum(
             "ihj,rjhe->rihe",
-            lax.all_gather(row_weights, "seq", axis=0, tiled=True),
+            collect(row_weights, "seq", 0),
             value_a,
             preferred_element_type=jnp.float32,
         )

time: 159 us -> 190 us (1.19)
  starting transfers between devices: 3.56 us -> 37 us
  blocking collectives: 36 us -> 15.5 us
  waiting for transfers between devices: 71.4 us -> 88.8 us
    ppermute x0 -> x15, starting transfers between devices: none -> 31.2 us  [the longest x7 31.1 us: collect(): upper.append(lax.ppermute(upper[-1] if upper else value, axis, back))]
    all_gather x1 -> x0, blocking collectives: 20.5 us -> none  [per_device(): lax.all_gather(row_weights, 'seq', axis=0, tiled=True)]
    ppermute x0 -> x15, waiting for transfers between devices: none -> 16.6 us  [the longest x8 15.5 us: collect(): lower.append(lax.ppermute(lower[-1] if lower else value, axis, pairs))]
    all_to_all x1, starting transfers between devices: 3.55 us -> 5.83 us  [per_device(): lax.all_to_all(normed_col, 'seq', split_axis=1, concat_axis=0, tiled=True)]
  transfers between devices with their start and end apart: 2 -> 17, of which waited for: 2 -> 13; matrix products, arithmetic and copies ran while one was open for 1% -> 1% of each run, Pallas kernels for 0% -> 0%
where the time goes in v1:
time: 190 us
  waiting for transfers between devices  88.8 us (47%)
  starting transfers between devices  37 us (19%)
  matrix products  18.1 us (10%)
  blocking collectives  15.5 us (8%)
  between operations  13.8 us (7%)
  local copies, waits for them, and re-layouts  11.1 us (6%)
  other arithmetic  5.58 us (3%)
    reduce_scatter x1, waiting for transfers between devices, per_device(): lax.psum_scatter(jnp.einsum('rihe,rjhe->ihj', query_a, key_a, preferred_e...  60.1 us
    ppermute x7, starting transfers between devices, collect(): upper.append(lax.ppermute(upper[-1] if upper else value, axis, back))  31.1 us
    all_to_all x1, blocking collectives, per_device(): lax.all_to_all(col_mixed, 'seq', split_axis=0, concat_axis=1, tiled=True)  15.5 us
    ppermute x8, waiting for transfers between devices, collect(): lower.append(lax.ppermute(lower[-1] if lower else value, axis, pairs))  15.5 us
    all_to_all x1, waiting for transfers between devices, per_device(): lax.all_to_all(normed_col, 'seq', split_axis=1, concat_axis=0, tiled=True)  12 us
    dot_general x6, matrix products, project(): jnp.dot(flattened, weight, preferred_element_type=jnp.float32)  7.94 us
    all_to_all x1, starting transfers between devices, per_device(): lax.all_to_all(normed_col, 'seq', split_axis=1, concat_axis=0, tiled=True)  5.83 us
    sub x1, matrix products, per_device(): col_weights = jax.nn.softmax(col_scores, axis=-1).astype(jnp.bfloat16)  4.24 us
  transfers between devices with their start and end apart: 17, of which 13 were waited for; matrix products, arithmetic and copies ran while one was open for 1% of the time, Pallas kernels for 0%

profile of v1, /device:TPU:0, one launch (start us, length us, event | category | flops | bytes accessed | tf_op | source)
XLA Modules:
  0.0 189.9 jit_solution(8460997103363839832)
XLA Ops:
  11.1 1.7 convolution_convert_fusion.4
  15.6 60.1 %reduce-scatter.2.cloned.1.call-done = f32[8,12,128]{2,1,0:T(8,128)} async-done(((f32[128,12,128]{2,1,0:T(8,128)}), f32[8,12,128]{2,1,0:T(8,128)}) %reduce-scatter.2.cloned.1.call-update) | async-done | bytes 49168 | tf_op jit(solution)/shard_map/reduce_scatter | solution.py:90
  76.9 6.0 %collective-permute-done = bf16[8,12,128]{2,1,0:T(8,128)(2,1)S(1)} collective-permute-done((bf16[8,12,128]{2,1,0:T(8,128)(2,1)S(1)}, bf16[8,12,128]{2,1,0:T(8,128)(2,1)S(1)}, u32[]{:S(2)}, u32[]{:S(2)}) %collective-permute-start) | collective-permute-done | bytes 24608 | tf_op jit(solution)/shard_map/ppermute | solution.py:23
  82.9 4.4 %collective-permute-start.8 = (bf16[8,12,128]{2,1,0:T(8,128)(2,1)S(1)}, bf16[8,12,128]{2,1,0:T(8,128)(2,1)S(1)}, u32[]{:S(2)}, u32[]{:S(2)}) collective-permute-start(bf16[8,12,128]{2,1,0:T(8,128)(2,1)S(1)} %fusion.15), channel_id=1, source_target_pairs={{1,0},{2,1},{3,2},{4,3},{5,4},{6,5},{7,6},{8,7},{9,8},{10,9},{11,1... | collective-permute-start | bytes 73736 | tf_op jit(solution)/shard_map/ppermute | solution.py:25
  87.3 1.6 collective-permute-done.1
  88.9 4.4 %collective-permute-start.9 = (bf16[8,12,128]{2,1,0:T(8,128)(2,1)S(1)}, bf16[8,12,128]{2,1,0:T(8,128)(2,1)S(1)}, u32[]{:S(2)}, u32[]{:S(2)}) collective-permute-start(bf16[8,12,128]{2,1,0:T(8,128)(2,1)S(1)} %collective-permute-done.8), channel_id=1, source_target_pairs={{1,0},{2,1},{3,2},{4,3},{5,4},{6,5},{7,6},{8,7},{9,8},{10,9},{11,1... | collective-permute-start | bytes 73736 | tf_op jit(solution)/shard_map/ppermute | solution.py:25
  93.4 1.6 collective-permute-done.2
  95.0 4.4 %collective-permute-start.10 = (bf16[8,12,128]{2,1,0:T(8,128)(2,1)S(1)}, bf16[8,12,128]{2,1,0:T(8,128)(2,1)S(1)}, u32[]{:S(2)}, u32[]{:S(2)}) collective-permute-start(bf16[8,12,128]{2,1,0:T(8,128)(2,1)S(1)} %collective-permute-done.9), channel_id=1, source_target_pairs={{1,0},{2,1},{3,2},{4,3},{5,4},{6,5},{7,6},{8,7},{9,8},{10,9},{11,1... | collective-permute-start | bytes 73736 | tf_op jit(solution)/shard_map/ppermute | solution.py:25
  99.4 1.6 collective-permute-done.3
  101.0 4.4 %collective-permute-start.11 = (bf16[8,12,128]{2,1,0:T(8,128)(2,1)S(1)}, bf16[8,12,128]{2,1,0:T(8,128)(2,1)S(1)}, u32[]{:S(2)}, u32[]{:S(2)}) collective-permute-start(bf16[8,12,128]{2,1,0:T(8,128)(2,1)S(1)} %collective-permute-done.10), channel_id=1, source_target_pairs={{1,0},{2,1},{3,2},{4,3},{5,4},{6,5},{7,6},{8,7},{9,8},{10,9},{11,1... | collective-permute-start | bytes 73736 | tf_op jit(solution)/shard_map/ppermute | solution.py:25
  105.4 1.6 collective-permute-done.4
  107.5 4.5 %collective-permute-start.12 = (bf16[8,12,128]{2,1,0:T(8,128)(2,1)S(1)}, bf16[8,12,128]{2,1,0:T(8,128)(2,1)S(1)}, u32[]{:S(2)}, u32[]{:S(2)}) collective-permute-start(bf16[8,12,128]{2,1,0:T(8,128)(2,1)S(1)} %collective-permute-done.11), channel_id=1, source_target_pairs={{1,0},{2,1},{3,2},{4,3},{5,4},{6,5},{7,6},{8,7},{9,8},{10,9},{11,1... | collective-permute-start | bytes 73736 | tf_op jit(solution)/shard_map/ppermute | solution.py:25
  113.6 4.4 %collective-permute-start.13 = (bf16[8,12,128]{2,1,0:T(8,128)(2,1)S(1)}, bf16[8,12,128]{2,1,0:T(8,128)(2,1)S(1)}, u32[]{:S(2)}, u32[]{:S(2)}) collective-permute-start(bf16[8,12,128]{2,1,0:T(8,128)(2,1)S(1)} %collective-permute-done.12), channel_id=1, source_target_pairs={{1,0},{2,1},{3,2},{4,3},{5,4},{6,5},{7,6},{8,7},{9,8},{10,9},{11,1... | collective-permute-start | bytes 73736 | tf_op jit(solution)/shard_map/ppermute | solution.py:25
  119.7 4.4 %collective-permute-start.14 = (bf16[8,12,128]{2,1,0:T(8,128)(2,1)S(1)}, bf16[8,12,128]{2,1,0:T(8,128)(2,1)S(1)}, u32[]{:S(2)}, u32[]{:S(2)}) collective-permute-start(bf16[8,12,128]{2,1,0:T(8,128)(2,1)S(1)} %collective-permute-done.13), channel_id=1, source_target_pairs={{1,0},{2,1},{3,2},{4,3},{5,4},{6,5},{7,6},{8,7},{9,8},{10,9},{11,1... | collective-permute-start | bytes 73736 | tf_op jit(solution)/shard_map/ppermute | solution.py:25
  129.5 5.8 %all-to-all-start = ((bf16[2,128,768]{2,0,1:T(2,128)(2,1)}), bf16[2,128,768]{2,0,1:T(2,128)(2,1)S(1)}, u32[]{:S(2)}, u32[]{:S(2)}) async-start(bf16[2,128,768]{2,0,1:T(2,128)(2,1)} %copy.130), calls=%async_computation.1 | async-start | bytes 786432 | tf_op jit(solution)/shard_map/all_to_all | solution.py:119
  135.5 12.0 %all-to-all-done = bf16[2,128,768]{2,0,1:T(2,128)(2,1)S(1)} async-done(((bf16[2,128,768]{2,0,1:T(2,128)(2,1)}), bf16[2,128,768]{2,0,1:T(2,128)(2,1)S(1)}, u32[]{:S(2)}, u32[]{:S(2)}) %all-to-all-start) | async-done | bytes 393248 | tf_op jit(solution)/shard_map/all_to_all | solution.py:119
  147.6 1.7 convolution_convert_fusion.2
  149.4 1.6 reshape_reshape.15
  151.0 1.7 convolution_convert_fusion.1
  154.3 1.7 convolution_convert_fusion.3
  157.6 4.2 %fusion.50 = (f32[8,12,32]{2,1,0:T(8,128)S(1)}, f32[8,12,32,32]{2,3,1,0:T(8,128)}) fusion(bf16[32,8,12,64]{3,2,1,0:T(8,128)(2,1)} %reshape_reshape.16, bf16[32,8,12,64]{3,2,1,0:T(8,128)(2,1)} %reshape_reshape.15, pred[8,32]{1,0:T(8,128)(4,1)S(1)} %iota_compare_fusion), kind=kOutput, calls=%fused_computation.97 | convolution fusion | flops 12976159 | bytes 1192192 | tf_op jit(solution)/shard_map/sub | solution.py:132
  161.9 2.1 %fusion.5 = bf16[32,8,12,64]{3,0,2,1:T(8,128)(2,1)S(1)} fusion(f32[8,12,32,32]{2,3,1,0:T(8,128)} %get-tuple-element.10, bf16[32,8,12,64]{3,2,1,0:T(8,128)(2,1)S(1)} %copy-done.4, f32[8,12,32]{2,1,0:T(8,128)S(1)} %get-tuple-element.9), kind=kOutput, calls=%fused_computation.9 | convolution fusion | flops 12976128 | bytes 1191936 | tf_op jit(solution)/shard_map/chrs,sche->rche/dot_general | solution.py:133
  165.0 15.5 %all_to_all.30 = bf16[32,8,768]{2,1,0:T(8,128)(2,1)S(1)} all-to-all(bf16[32,8,768]{2,1,0:T(8,128)(2,1)S(1)} %reshape.197), channel_id=1, replica_groups=mesh['grp'=2,'seq'=16] {'seq'}, dimensions={0} | all-to-all | bytes 786432 | tf_op jit(solution)/shard_map/all_to_all | solution.py:137
  180.5 2.5 %fusion.8 = bf16[2,128,768]{2,1,0:T(8,128)(2,1)} fusion(f32[2,128,768]{2,1,0:T(8,128)S(1)} %get-tuple-element.8, bf16[768,768]{1,0:T(8,128)(2,1)} %param.25, bf16[2,16,8,768]{3,2,0,1:T(8,128)(2,1)S(1)} %bitcast.92), kind=kOutput, calls=%fused_computation.15 | convolution fusion | flops 302383104 | bytes 2752512 | tf_op jit(solution)/shard_map/dot_general | solution.py:138
  (94 shorter events, 21.6 us)
Async XLA Ops:
  6.5 120.2 %copy-start = (bf16[768,768]{1,0:T(8,128)(2,1)S(1)}, bf16[768,768]{1,0:T(8,128)(2,1)}, u32[]{:S(2)}) copy-start(bf16[768,768]{1,0:T(8,128)(2,1)} %param.20) | copy-start | bytes 3538948
  6.5 3.8 %copy-start.2 = (bf16[768,768]{1,0:T(8,128)(2,1)S(1)}, bf16[768,768]{1,0:T(8,128)(2,1)}, u32[]{:S(2)}) copy-start(bf16[768,768]{1,0:T(8,128)(2,1)} %param.18) | copy-start | bytes 3538948
  6.5 69.2 %reduce-scatter.2.cloned.1.call-start = ((), (), s32[]{:S(2)}) async-start(), calls=%async_computation.3 | async-start | bytes 1114112 | tf_op jit(solution)/shard_map/reduce_scatter | solution.py:90
  12.9 0.7 copy-start.7
  14.1 93.0 %copy-start.3 = (bf16[768,768]{1,0:T(8,128)(2,1)S(1)}, bf16[768,768]{1,0:T(8,128)(2,1)}, u32[]{:S(2)}) copy-start(bf16[768,768]{1,0:T(8,128)(2,1)} %param.19) | copy-start | bytes 3538948
  76.8 6.1 %collective-permute-start = (bf16[8,12,128]{2,1,0:T(8,128)(2,1)S(1)}, bf16[8,12,128]{2,1,0:T(8,128)(2,1)S(1)}, u32[]{:S(2)}, u32[]{:S(2)}) collective-permute-start(bf16[8,12,128]{2,1,0:T(8,128)(2,1)S(1)} %fusion.15), channel_id=1, source_target_pairs={{0,1},{1,2},{2,3},{3,4},{4,5},{5,6},{6,7},{7,8},{8,9},{9,10},{10,1... | collective-permute-start | bytes 73736 | tf_op jit(solution)/shard_map/ppermute | solution.py:23
  82.9 6.0 %collective-permute-start.1 = (bf16[8,12,128]{2,1,0:T(8,128)(2,1)S(1)}, bf16[8,12,128]{2,1,0:T(8,128)(2,1)S(1)}, u32[]{:S(2)}, u32[]{:S(2)}) collective-permute-start(bf16[8,12,128]{2,1,0:T(8,128)(2,1)S(1)} %collective-permute-done), channel_id=1, source_target_pairs={{0,1},{1,2},{2,3},{3,4},{4,5},{5,6},{6,7},{7,8},{8,9},{9,10},{10,1... | collective-permute-start | bytes 73736 | tf_op jit(solution)/shard_map/ppermute | solution.py:23
  82.9 6.0 %collective-permute-start.8 = (bf16[8,12,128]{2,1,0:T(8,128)(2,1)S(1)}, bf16[8,12,128]{2,1,0:T(8,128)(2,1)S(1)}, u32[]{:S(2)}, u32[]{:S(2)}) collective-permute-start(bf16[8,12,128]{2,1,0:T(8,128)(2,1)S(1)} %fusion.15), channel_id=1, source_target_pairs={{1,0},{2,1},{3,2},{4,3},{5,4},{6,5},{7,6},{8,7},{9,8},{10,9},{11,1... | collective-permute-start | bytes 73736 | tf_op jit(solution)/shard_map/ppermute | solution.py:25
  88.9 6.0 %collective-permute-start.2 = (bf16[8,12,128]{2,1,0:T(8,128)(2,1)S(1)}, bf16[8,12,128]{2,1,0:T(8,128)(2,1)S(1)}, u32[]{:S(2)}, u32[]{:S(2)}) collective-permute-start(bf16[8,12,128]{2,1,0:T(8,128)(2,1)S(1)} %collective-permute-done.1), channel_id=1, source_target_pairs={{0,1},{1,2},{2,3},{3,4},{4,5},{5,6},{6,7},{7,8},{8,9},{9,10},{10,1... | collective-permute-start | bytes 73736 | tf_op jit(solution)/shard_map/ppermute | solution.py:23
  88.9 6.0 %collective-permute-start.9 = (bf16[8,12,128]{2,1,0:T(8,128)(2,1)S(1)}, bf16[8,12,128]{2,1,0:T(8,128)(2,1)S(1)}, u32[]{:S(2)}, u32[]{:S(2)}) collective-permute-start(bf16[8,12,128]{2,1,0:T(8,128)(2,1)S(1)} %collective-permute-done.8), channel_id=1, source_target_pairs={{1,0},{2,1},{3,2},{4,3},{5,4},{6,5},{7,6},{8,7},{9,8},{10,9},{11,1... | collective-permute-start | bytes 73736 | tf_op jit(solution)/shard_map/ppermute | solution.py:25
  95.0 6.0 %collective-permute-start.3 = (bf16[8,12,128]{2,1,0:T(8,128)(2,1)S(1)}, bf16[8,12,128]{2,1,0:T(8,128)(2,1)S(1)}, u32[]{:S(2)}, u32[]{:S(2)}) collective-permute-start(bf16[8,12,128]{2,1,0:T(8,128)(2,1)S(1)} %collective-permute-done.2), channel_id=1, source_target_pairs={{0,1},{1,2},{2,3},{3,4},{4,5},{5,6},{6,7},{7,8},{8,9},{9,10},{10,1... | collective-permute-start | bytes 73736 | tf_op jit(solution)/shard_map/ppermute | solution.py:23
  95.0 6.0 %collective-permute-start.10 = (bf16[8,12,128]{2,1,0:T(8,128)(2,1)S(1)}, bf16[8,12,128]{2,1,0:T(8,128)(2,1)S(1)}, u32[]{:S(2)}, u32[]{:S(2)}) collective-permute-start(bf16[8,12,128]{2,1,0:T(8,128)(2,1)S(1)} %collective-permute-done.9), channel_id=1, source_target_pairs={{1,0},{2,1},{3,2},{4,3},{5,4},{6,5},{7,6},{8,7},{9,8},{10,9},{11,1... | collective-permute-start | bytes 73736 | tf_op jit(solution)/shard_map/ppermute | solution.py:25
  101.0 6.0 %collective-permute-start.4 = (bf16[8,12,128]{2,1,0:T(8,128)(2,1)S(1)}, bf16[8,12,128]{2,1,0:T(8,128)(2,1)S(1)}, u32[]{:S(2)}, u32[]{:S(2)}) collective-permute-start(bf16[8,12,128]{2,1,0:T(8,128)(2,1)S(1)} %collective-permute-done.3), channel_id=1, source_target_pairs={{0,1},{1,2},{2,3},{3,4},{4,5},{5,6},{6,7},{7,8},{8,9},{9,10},{10,1... | collective-permute-start | bytes 73736 | tf_op jit(solution)/shard_map/ppermute | solution.py:23
  101.0 6.5 %collective-permute-start.11 = (bf16[8,12,128]{2,1,0:T(8,128)(2,1)S(1)}, bf16[8,12,128]{2,1,0:T(8,128)(2,1)S(1)}, u32[]{:S(2)}, u32[]{:S(2)}) collective-permute-start(bf16[8,12,128]{2,1,0:T(8,128)(2,1)S(1)} %collective-permute-done.10), channel_id=1, source_target_pairs={{1,0},{2,1},{3,2},{4,3},{5,4},{6,5},{7,6},{8,7},{9,8},{10,9},{11,1... | collective-permute-start | bytes 73736 | tf_op jit(solution)/shard_map/ppermute | solution.py:25
  107.0 6.0 %collective-permute-start.5 = (bf16[8,12,128]{2,1,0:T(8,128)(2,1)S(1)}, bf16[8,12,128]{2,1,0:T(8,128)(2,1)S(1)}, u32[]{:S(2)}, u32[]{:S(2)}) collective-permute-start(bf16[8,12,128]{2,1,0:T(8,128)(2,1)S(1)} %collective-permute-done.4), channel_id=1, source_target_pairs={{0,1},{1,2},{2,3},{3,4},{4,5},{5,6},{6,7},{7,8},{8,9},{9,10},{10,1... | collective-permute-start | bytes 73736 | tf_op jit(solution)/shard_map/ppermute | solution.py:23
  107.5 6.1 %collective-permute-start.12 = (bf16[8,12,128]{2,1,0:T(8,128)(2,1)S(1)}, bf16[8,12,128]{2,1,0:T(8,128)(2,1)S(1)}, u32[]{:S(2)}, u32[]{:S(2)}) collective-permute-start(bf16[8,12,128]{2,1,0:T(8,128)(2,1)S(1)} %collective-permute-done.11), channel_id=1, source_target_pairs={{1,0},{2,1},{3,2},{4,3},{5,4},{6,5},{7,6},{8,7},{9,8},{10,9},{11,1... | collective-permute-start | bytes 73736 | tf_op jit(solution)/shard_map/ppermute | solution.py:25
  113.1 6.0 %collective-permute-start.6 = (bf16[8,12,128]{2,1,0:T(8,128)(2,1)S(1)}, bf16[8,12,128]{2,1,0:T(8,128)(2,1)S(1)}, u32[]{:S(2)}, u32[]{:S(2)}) collective-permute-start(bf16[8,12,128]{2,1,0:T(8,128)(2,1)S(1)} %collective-permute-done.5), channel_id=1, source_target_pairs={{0,1},{1,2},{2,3},{3,4},{4,5},{5,6},{6,7},{7,8},{8,9},{9,10},{10,1... | collective-permute-start | bytes 73736 | tf_op jit(solution)/shard_map/ppermute | solution.py:23
  113.6 6.0 %collective-permute-start.13 = (bf16[8,12,128]{2,1,0:T(8,128)(2,1)S(1)}, bf16[8,12,128]{2,1,0:T(8,128)(2,1)S(1)}, u32[]{:S(2)}, u32[]{:S(2)}) collective-permute-start(bf16[8,12,128]{2,1,0:T(8,128)(2,1)S(1)} %collective-permute-done.12), channel_id=1, source_target_pairs={{1,0},{2,1},{3,2},{4,3},{5,4},{6,5},{7,6},{8,7},{9,8},{10,9},{11,1... | collective-permute-start | bytes 73736 | tf_op jit(solution)/shard_map/ppermute | solution.py:25
  119.1 6.0 %collective-permute-start.7 = (bf16[8,12,128]{2,1,0:T(8,128)(2,1)S(1)}, bf16[8,12,128]{2,1,0:T(8,128)(2,1)S(1)}, u32[]{:S(2)}, u32[]{:S(2)}) collective-permute-start(bf16[8,12,128]{2,1,0:T(8,128)(2,1)S(1)} %collective-permute-done.6), channel_id=1, source_target_pairs={{0,1},{1,2},{2,3},{3,4},{4,5},{5,6},{6,7},{7,8},{8,9},{9,10},{10,1... | collective-permute-start | bytes 73736 | tf_op jit(solution)/shard_map/ppermute | solution.py:23
  119.7 6.0 %collective-permute-start.14 = (bf16[8,12,128]{2,1,0:T(8,128)(2,1)S(1)}, bf16[8,12,128]{2,1,0:T(8,128)(2,1)S(1)}, u32[]{:S(2)}, u32[]{:S(2)}) collective-permute-start(bf16[8,12,128]{2,1,0:T(8,128)(2,1)S(1)} %collective-permute-done.13), channel_id=1, source_target_pairs={{1,0},{2,1},{3,2},{4,3},{5,4},{6,5},{7,6},{8,7},{9,8},{10,9},{11,1... | collective-permute-start | bytes 73736 | tf_op jit(solution)/shard_map/ppermute | solution.py:25
  126.3 1.0 copy-start.1
  127.3 0.8 copy-start.5
  129.5 18.0 %all-to-all-start = ((bf16[2,128,768]{2,0,1:T(2,128)(2,1)}), bf16[2,128,768]{2,0,1:T(2,128)(2,1)S(1)}, u32[]{:S(2)}, u32[]{:S(2)}) async-start(bf16[2,128,768]{2,0,1:T(2,128)(2,1)} %copy.130), calls=%async_computation.1 | async-start | bytes 786432 | tf_op jit(solution)/shard_map/all_to_all | solution.py:119
  157.6 4.2 %copy-start.4 = (bf16[32,8,12,64]{3,2,1,0:T(8,128)(2,1)S(1)}, bf16[32,8,12,64]{3,2,1,0:T(8,128)(2,1)}, u32[]{:S(2)}) copy-start(bf16[32,8,12,64]{3,2,1,0:T(8,128)(2,1)} %reshape_reshape.14) | copy-start | bytes 1179652
  (1 other events, 0.7 us)
Sparse Core Ops, SparseCore 0:
  15.6 60.1 reduce-scatter.1
